TPU v7x, 256 devices: a whole 4x4x8 slice. The times are simulated.
256 devices in a mesh: lat: 16 (over y_lo, x, core), lon: 16 (over y_hi, z).
Axes of the slice: x: 4, y: 4 (y_hi: 2, y_lo: 2; y = y_hi * 2 + y_lo), z: 8, core: 2. Of those that a mesh axis runs over, the one named last changes fastest.
Arguments:
- fields: bfloat16 [32, 128, 4096], P(None, 'lat', 'lon'), may hold values from -6 to 6
- cotangent: bfloat16 [32, 128, 4096], P(None, 'lat', 'lon'), may hold values from -0.008239746 to 0.008239746
- kernel_in: bfloat16 [9, 128, 32], replicated, may hold values from -0.375 to 0.375
- kernel_mid: bfloat16 [9, 128, 128], replicated, may hold values from -0.1875 to 0.1875
- kernel_out: bfloat16 [9, 32, 128], replicated, may hold values from -0.1875 to 0.1875
- patch_anchors: int32 [16, 16, 4, 2], P('lat', 'lon'), may hold values from 0 to 8
- blend_weights: int32 [4, 128, 4096], P(None, 'lat', 'lon'), may hold values from 1 to 8
- tile_counts: int32 [16, 16], P('lat', 'lon'), may hold values from 0 to 4, as said below
Outputs:
- blended: float32 [32, 128, 4096], P(None, 'lat', 'lon')
- grad_in: float32 [9, 128, 32], replicated
- grad_mid: float32 [9, 128, 128], replicated
- grad_out: float32 [9, 32, 128], replicated
Inputs may be any that keep to these rules, and one draw needn't show every extreme that they name: `tile_counts`: the counts of the tiles in lat rows i and i + 8 at the same lon sum to exactly 4; tile (1, 0) holds 4 patches and tile (9, 0) none.
All inputs are finite; a program needn't handle non-finite values.
Results may differ from a plain program's by a relative error of at most 0.005.
Values may be sent and summed in bfloat16 or wider, within the bound.
A program may use at most 64 MiB of HBM per device.

v0:
```python
import jax
import jax.numpy as jnp
from jax import lax
from jax.sharding import PartitionSpec as P

MARGIN = 4
SLOTS = 4
KERNEL_TAPS = ((0, 0), (0, 1), (0, 2), (1, 0), (1, 1), (1, 2), (2, 0), (2, 1), (2, 2))


def extended_2(block, sides, width):
    for axis, dim in sides:
        count = lax.axis_size(axis)
        forward = [(i, i + 1) for i in range(count - 1)]
        forward.append((count - 1, 0))
        backward = [(target, source) for source, target in forward]
        low = lax.ppermute(
            lax.slice_in_dim(block, block.shape[dim] - width, None, axis=dim), axis, forward
        )
        high = lax.ppermute(lax.slice_in_dim(block, 0, width, axis=dim), axis, backward)
        block = jnp.concatenate([low, block, high], axis=dim)
    return block


def shifted(value, axis, steps):
    count = lax.axis_size(axis)
    pairs = [(source, (source + steps) % count) for source in range(count)]
    return lax.ppermute(value, axis, pairs)


def forward_conv(values, kernel):
    height, breadth = (values.shape[1], values.shape[2])
    padded = jnp.pad(values, ((0, 0), (1, 1), (1, 1)))
    summed = jnp.zeros((kernel.shape[1], height, breadth), jnp.float32)
    for tap_index, (tap_row, tap_col) in enumerate(KERNEL_TAPS):
        summed = summed + jnp.einsum(
            "ok,khw->ohw",
            kernel[tap_index],
            padded[:, tap_row : tap_row + height, tap_col : tap_col + breadth],
            preferred_element_type=jnp.float32,
        )
    return summed


def backward_conv(cotangent, kernel):
    height, breadth = (cotangent.shape[1], cotangent.shape[2])
    padded = jnp.pad(cotangent, ((0, 0), (1, 1), (1, 1)))
    summed = jnp.zeros((kernel.shape[2], height, breadth), jnp.float32)
    for tap_index, (tap_row, tap_col) in enumerate(KERNEL_TAPS):
        summed = summed + jnp.einsum(
            "ok,ohw->khw",
            kernel[tap_index],
            padded[:, 2 - tap_row : 2 - tap_row + height, 2 - tap_col : 2 - tap_col + breadth],
            preferred_element_type=jnp.float32,
        )
    return summed


def kernel_grad(cotangent, values):
    height, breadth = (values.shape[1], values.shape[2])
    padded = jnp.pad(values, ((0, 0), (1, 1), (1, 1)))
    pieces = [
        jnp.einsum(
            "ohw,khw->ok",
            cotangent,
            padded[:, tap_row : tap_row + height, tap_col : tap_col + breadth],
            preferred_element_type=jnp.float32,
        )
        for tap_row, tap_col in KERNEL_TAPS
    ]
    return jnp.stack(pieces)


def silu_slope(pre_act):
    sigmoid = jax.nn.sigmoid(pre_act)
    return sigmoid * (1.0 + pre_act * (1.0 - sigmoid))


def patch_pass(inputs, out_grad, kernel_in, kernel_mid, kernel_out):
    pre_one = forward_conv(inputs, kernel_in)
    hidden_one = jax.nn.silu(pre_one).astype(jnp.bfloat16)
    pre_two = forward_conv(hidden_one, kernel_mid)
    hidden_two = (hidden_one.astype(jnp.float32) + jax.nn.silu(pre_two)).astype(jnp.bfloat16)
    result = forward_conv(hidden_two, kernel_out)
    grad_two = backward_conv(out_grad, kernel_out)
    delta_two = (grad_two * silu_slope(pre_two)).astype(jnp.bfloat16)
    grad_one = grad_two + backward_conv(delta_two, kernel_mid)
    delta_one = (grad_one * silu_slope(pre_one)).astype(jnp.bfloat16)
    return (
        result,
        kernel_grad(delta_one, inputs),
        kernel_grad(delta_two, hidden_one),
        kernel_grad(out_grad, hidden_two),
    )


def run_patches(inputs, out_grads, kernel_in, kernel_mid, kernel_out):
    initial = (
        jnp.zeros(kernel_in.shape, jnp.float32),
        jnp.zeros(kernel_mid.shape, jnp.float32),
        jnp.zeros(kernel_out.shape, jnp.float32),
    )

    def step_patch(running, slot_pair):
        result, part_in, part_mid, part_out = patch_pass(
            slot_pair[0], slot_pair[1], kernel_in, kernel_mid, kernel_out
        )
        return ((running[0] + part_in, running[1] + part_mid, running[2] + part_out), result)

    return lax.scan(step_patch, initial, (inputs, out_grads))


def fold_canvas(canvas, keep_top, keep_bottom):
    extended = extended_2(canvas, (("lat", 1), ("lon", 2)), MARGIN)
    height = canvas.shape[1] - 2 * MARGIN
    breadth = canvas.shape[2] - 2 * MARGIN
    inner_rows = slice(2 * MARGIN, 2 * MARGIN + height)
    inner_cols = slice(2 * MARGIN, 2 * MARGIN + breadth)
    center_part = extended[:, inner_rows, inner_cols]
    col_left = ((0, 0), (0, 0), (0, breadth - MARGIN))
    col_right = ((0, 0), (0, 0), (breadth - MARGIN, 0))
    upper_part = (
        extended[:, :MARGIN, inner_cols]
        + jnp.pad(extended[:, :MARGIN, :MARGIN], col_left)
        + jnp.pad(extended[:, :MARGIN, -MARGIN:], col_right)
    )
    lower_part = (
        extended[:, -MARGIN:, inner_cols]
        + jnp.pad(extended[:, -MARGIN:, :MARGIN], col_left)
        + jnp.pad(extended[:, -MARGIN:, -MARGIN:], col_right)
    )
    summed = (
        center_part
        + jnp.pad(extended[:, inner_rows, :MARGIN], col_left)
        + jnp.pad(extended[:, inner_rows, -MARGIN:], col_right)
    )
    summed = summed + jnp.pad(upper_part * keep_top, ((0, 0), (0, height - MARGIN), (0, 0)))
    summed = summed + jnp.pad(lower_part * keep_bottom, ((0, 0), (height - MARGIN, 0), (0, 0)))
    return summed


def shards(
    fields, cotangent, kernel_in, kernel_mid, kernel_out, patch_anchors, blend_weights, tile_counts
):
    channels, height, breadth = (fields.shape[0], fields.shape[1], fields.shape[2])
    canvas_rows = height + 2 * MARGIN
    canvas_cols = breadth + 2 * MARGIN
    lat_size = lax.axis_size("lat")
    lat_index = lax.axis_index("lat")
    keep_top = (lat_index > 0).astype(jnp.float32)
    keep_bottom = (lat_index < lat_size - 1).astype(jnp.float32)
    slot_count = tile_counts[0, 0]
    slot_live = (jnp.arange(SLOTS) < slot_count).astype(jnp.int32)
    weights = (blend_weights * slot_live[:, None, None]).astype(jnp.float32)
    starts = patch_anchors[0, 0]

    def place_slots(per_slot):
        canvas = jnp.zeros((per_slot.shape[1], canvas_rows, canvas_cols), jnp.float32)
        for slot_index in range(SLOTS):
            corner = (jnp.int32(0), starts[slot_index, 0], starts[slot_index, 1])
            current = lax.dynamic_slice(canvas, corner, per_slot.shape[1:])
            canvas = lax.dynamic_update_slice(canvas, current + per_slot[slot_index], corner)
        return canvas

    total_weight = jnp.maximum(
        fold_canvas(place_slots(weights[:, None]), keep_top, keep_bottom), 1.0
    )
    scaled = (cotangent.astype(jnp.float32) / total_weight).astype(jnp.bfloat16)
    wide_fields, wide_scaled = (
        extended_2(fields, (("lat", 1), ("lon", 2)), MARGIN),
        extended_2(scaled, (("lat", 1), ("lon", 2)), MARGIN),
    )
    row_ids = jnp.arange(canvas_rows)[None, :, None]
    keep_rows = ((row_ids >= MARGIN) | (keep_top > 0.0)) & (
        (row_ids < height + MARGIN) | (keep_bottom > 0.0)
    )
    wide_fields = jnp.where(keep_rows, wide_fields, jnp.zeros_like(wide_fields))
    wide_scaled = jnp.where(keep_rows, wide_scaled, jnp.zeros_like(wide_scaled))
    window_list = []
    grad_list = []
    for slot_index in range(SLOTS):
        corner = (jnp.int32(0), starts[slot_index, 0], starts[slot_index, 1])
        window_list.append(lax.dynamic_slice(wide_fields, corner, (channels, height, breadth)))
        scaled_window = lax.dynamic_slice(wide_scaled, corner, (channels, height, breadth)).astype(
            jnp.float32
        )
        grad_list.append((weights[slot_index] * scaled_window).astype(jnp.bfloat16))
    inputs = jnp.stack(window_list)
    out_grads = jnp.stack(grad_list)
    half_slots = SLOTS // 2
    upper_half = (lat_index >= lat_size // 2).astype(jnp.int32)
    first_count = jnp.where(upper_half == 0, slot_count, SLOTS - slot_count)
    outgoing_inputs = jnp.where(upper_half == 0, inputs[half_slots:], inputs[:half_slots])
    outgoing_grads = jnp.where(upper_half == 0, out_grads[half_slots:], out_grads[:half_slots])
    incoming_inputs, incoming_grads = shifted(
        (outgoing_inputs, outgoing_grads), "lat", lat_size // 2
    )
    table_inputs = jnp.concatenate([inputs, incoming_inputs], axis=0)
    table_grads = jnp.concatenate([out_grads, incoming_grads], axis=0)
    position = upper_half * half_slots + jnp.arange(half_slots, dtype=jnp.int32)
    picked = jnp.where(
        position < first_count,
        jnp.where(upper_half == 0, position, position + SLOTS - half_slots),
        jnp.where(upper_half == 0, SLOTS + position - first_count, position - first_count),
    )
    picked = jnp.clip(picked, 0, SLOTS + half_slots - 1)
    totals, computed = run_patches(
        jnp.take(table_inputs, picked, axis=0),
        jnp.take(table_grads, picked, axis=0),
        kernel_in,
        kernel_mid,
        kernel_out,
    )
    returned = shifted(computed, "lat", lat_size // 2)
    ordered = jnp.where(
        upper_half == 0,
        jnp.concatenate([computed, returned], axis=0),
        jnp.concatenate([returned, computed], axis=0),
    )
    where_slot = jnp.clip(
        jnp.arange(SLOTS, dtype=jnp.int32) + upper_half * first_count, 0, SLOTS - 1
    )
    outputs = jnp.take(ordered, where_slot, axis=0)
    weighted = weights[:, None] * outputs
    numerator = fold_canvas(place_slots(weighted), keep_top, keep_bottom)
    blended = numerator / total_weight
    summed_grads = lax.psum((totals[0], totals[1], totals[2]), ("lat", "lon"))
    return (blended, summed_grads[0], summed_grads[1], summed_grads[2])


def solution(mesh):
    return jax.shard_map(
        shards,
        mesh=mesh,
        in_specs=(
            P(None, "lat", "lon"),
            P(None, "lat", "lon"),
            P(),
            P(),
            P(),
            P("lat", "lon", None, None),
            P(None, "lat", "lon"),
            P("lat", "lon"),
        ),
        out_specs=(P(None, "lat", "lon"), P(), P(), P()),
        check_vma=False,
    )
```

profile of v0, /device:TPU:1, one launch (start us, length us, event | category | flops | bytes accessed | tf_op | source)
XLA Modules:
  0.0 498.2 jit_solution(12220531734381858021)
XLA Ops:
  27.7 2.6 collective-permute-start
  31.2 3.8 collective-permute-start.10
  35.4 7.0 %collective-permute-start.3 = (f32[1,24,4]{2,1,0:T(8,128)S(1)}, f32[1,24,4]{2,1,0:T(8,128)S(1)}, u32[]{:S(2)}, u32[]{:S(2)}) collective-permute-start(f32[1,24,4]{2,1,0:T(8,128)S(1)} %get-tuple-element.254), channel_id=1, source_target_pairs={{1,0},{2,1},{3,2},{4,3},{5,4},{6,5},{7,6},{8,7},{9,8},{10,9},{11,1... | collective-permute-start | bytes 1160 | tf_op jit(solution)/shard_map/ppermute | solution.py:20
  42.4 1.0 collective-permute-done.2
  46.1 5.5 %collective-permute-start.12 = (bf16[32,16,4]{2,1,0:T(8,128)(2,1)S(1)}, bf16[32,16,4]{2,1,0:T(8,128)(2,1)S(1)}, u32[]{:S(2)}, u32[]{:S(2)}) collective-permute-start(bf16[32,16,4]{2,1,0:T(8,128)(2,1)S(1)} %get-tuple-element.246), channel_id=1, source_target_pairs={{1,0},{2,1},{3,2},{4,3},{5,4},{6,5},{7,6},{8,7},{9,8},{10,9},{11,1... | collective-permute-start | bytes 12296 | tf_op jit(solution)/shard_map/ppermute | solution.py:20
  52.0 18.8 %collective-permute-start.7 = (bf16[32,16,4]{2,1,0:T(8,128)(2,1)S(1)}, bf16[32,16,4]{2,1,0:T(8,128)(2,1)S(1)}, u32[]{:S(2)}, u32[]{:S(2)}) collective-permute-start(bf16[32,16,4]{2,1,0:T(8,128)(2,1)S(1)} %get-tuple-element.248), channel_id=1, source_target_pairs={{1,0},{2,1},{3,2},{4,3},{5,4},{6,5},{7,6},{8,7},{9,8},{10,9},{11,1... | collective-permute-start | bytes 12296 | tf_op jit(solution)/shard_map/ppermute | solution.py:20
  70.8 1.9 collective-permute-done.7
  72.7 1.0 maximum_select_fusion.2
  76.7 3.1 collective-permute-done.8
  80.4 2.2 collective-permute-done.13
  84.2 72.5 %while.19 = (s32[]{:T(128)}, f32[9,128,32]{1,2,0:T(8,128)S(1)}, f32[9,128,128]{2,1,0:T(8,128)S(1)}, f32[9,32,128]{2,1,0:T(8,128)}, f32[2,32,8,256]{3,2,1,0:T(8,1...) while((s32[]{:T(128)}, f32[9,128,32]{1,2,0:T(8,128)S(1)}, ...), condition=%wide.region_1.3_spmd.clone, body=%wide.region_0.2_spmd.clone.sunk | while | flops 2583609344 | bytes 133587216 | solution.py:110
  84.2 1.0 constant_dynamic-slice_fusion.3
  88.7 1.6 multiply_convert_fusion.8
  100.9 0.8 fusion.448
  102.6 0.8 fusion.450
  103.4 0.9 fusion.451
  105.1 0.9 fusion.453
  105.9 0.8 fusion.454
  107.6 0.8 fusion.456
  108.5 1.6 select_add_fusion.8
  115.7 0.9 copy-done.20
  119.5 0.9 copy-done.5
  120.4 1.0 constant_dynamic-slice_fusion.3
  124.9 1.6 multiply_convert_fusion.8
  137.1 0.8 fusion.448
  138.8 0.8 fusion.450
  139.6 0.9 fusion.451
  141.3 0.9 fusion.453
  142.2 0.8 fusion.454
  143.8 0.8 fusion.456
  144.7 1.7 select_add_fusion.8
  152.0 0.9 copy-done.20
  155.8 0.9 copy-done.5
  157.5 7.5 %collective-permute-done.14 = f32[2,32,8,256]{3,2,1,0:T(8,128)S(1)} collective-permute-done((f32[2,32,8,256]{3,2,1,0:T(8,128)}, f32[2,32,8,256]{3,2,1,0:T(8,128)S(1)}, u32[]{:S(2)}, u32[]{:S(2)}) %collective-permute-start.14) | collective-permute-done | bytes 524320 | tf_op jit(solution)/shard_map/ppermute | solution.py:28
  165.0 1.3 maximum_select_fusion
  167.3 10.2 %dynamic_update_slice.35 = f32[32,16,264]{2,1,0:T(8,128)S(1)} dynamic-update-slice(f32[32,16,264]{2,1,0:T(8,128)S(1)} %broadcast_in_dim.59, f32[32,8,256]{2,1,0:T(8,128)S(1)} %slice_bitcast_fusion.3, s32[]{:T(128)} %constant.84.clone.1, s32[]{:T(128)S(6)} %select_n.136, s32[]{:T(128)S(6)} %select_n.137) | dynamic-update-slice | bytes 524292 | tf_op jit(solution)/shard_map/dynamic_update_slice | solution.py:162
  177.6 10.2 %dynamic_update_slice.36 = f32[32,16,264]{2,1,0:T(8,128)S(1)} dynamic-update-slice(f32[32,16,264]{2,1,0:T(8,128)S(1)} %dynamic_update_slice.35, f32[32,8,256]{2,1,0:T(8,128)S(1)} %fusion.200, s32[]{:T(128)} %constant.84.clone.1, s32[]{:T(128)S(6)} %select_n.138, s32[]{:T(128)S(6)} %select_n.139) | dynamic-update-slice | bytes 524292 | tf_op jit(solution)/shard_map/dynamic_update_slice | solution.py:162
  188.0 1.3 dynamic_update_slice.37
  189.4 10.2 %dynamic_update_slice.38 = f32[32,16,264]{2,1,0:T(8,128)S(1)} dynamic-update-slice(f32[32,16,264]{2,1,0:T(8,128)S(1)} %dynamic_update_slice.37, f32[32,8,256]{2,1,0:T(8,128)S(1)} %fusion.198, s32[]{:T(128)} %constant.84.clone.1, s32[]{:T(128)S(6)} %select_n.142, s32[]{:T(128)S(6)} %select_n.143) | dynamic-update-slice | bytes 524292 | tf_op jit(solution)/shard_map/dynamic_update_slice | solution.py:162
  199.6 9.2 %collective-permute-start.15 = (f32[32,4,264]{2,1,0:T(4,128)S(1)}, f32[32,4,264]{2,1,0:T(4,128)S(1)}, u32[]{:S(2)}, u32[]{:S(2)}) collective-permute-start(f32[32,4,264]{2,1,0:T(4,128)S(1)} %get-tuple-element.239), channel_id=1, source_target_pairs={{0,16},{16,32},{32,48},{48,64},{64,80},{80,96},{96,112},{112,128},... | collective-permute-start | bytes 405512 | tf_op jit(solution)/shard_map/ppermute | solution.py:17
  208.8 2.6 collective-permute-done.15
  211.4 6.6 %collective-permute-done.16 = f32[32,4,264]{2,1,0:T(4,128)S(1)} collective-permute-done((f32[32,4,264]{2,1,0:T(4,128)S(1)}, f32[32,4,264]{2,1,0:T(4,128)S(1)}, u32[]{:S(2)}, u32[]{:S(2)}) %collective-permute-start.16) | collective-permute-done | bytes 135200 | tf_op jit(solution)/shard_map/ppermute | solution.py:20
  218.4 11.1 %collective-permute-start.18 = (f32[32,24,4]{2,1,0:T(8,128)S(1)}, f32[32,24,4]{2,1,0:T(8,128)S(1)}, u32[]{:S(2)}, u32[]{:S(2)}) collective-permute-start(f32[32,24,4]{2,1,0:T(8,128)S(1)} %get-tuple-element.238), channel_id=1, source_target_pairs={{1,0},{2,1},{3,2},{4,3},{5,4},{6,5},{7,6},{8,7},{9,8},{10,9},{11,1... | collective-permute-start | bytes 36872 | tf_op jit(solution)/shard_map/ppermute | solution.py:20
  229.4 5.5 %collective-permute-done.17 = f32[32,24,4]{2,1,0:T(8,128)S(1)} collective-permute-done((f32[32,24,4]{2,1,0:T(8,128)S(1)}, f32[32,24,4]{2,1,0:T(8,128)S(1)}, u32[]{:S(2)}, u32[]{:S(2)}) %collective-permute-start.17) | collective-permute-done | bytes 12320 | tf_op jit(solution)/shard_map/ppermute | solution.py:17
  237.6 0.9 fusion.197
  238.5 248.2 %all-reduce.24.cloned.1.call-done = (f32[9,128,32]{1,2,0:T(8,128)}, f32[9,128,128]{2,1,0:T(8,128)}, f32[9,32,128]{2,1,0:T(8,128)}) async-done(((f32[9,128,32]{1,2,0:T(8,128)}, f32[9,128,128]{2,1,0:T(8,128)}, f32[9,32,128]{2,1,0:T(8,128)}), (f32[9,128,32]{1,2,0:T(8,128)}, f32[9,128,128]{2,1,0:T(8,128)}, f32[9,32,128]{2,1,0:T(8,128)})) %all-reduce.24.cloned.1.call-update) | async-done | bytes 884752 | tf_op jit(solution)/shard_map/psum | solution.py:227
  486.7 1.6 copy.283
  488.3 2.0 copy.284
  (283 shorter events, 69.2 us)
Async XLA Ops:
  7.2 0.7 copy-start.19
  7.2 479.6 %all-reduce.24.cloned.1.call-start = ((), (), s32[]{:S(2)}) async-start(), calls=%async_computation | async-start | bytes 1769472 | tf_op jit(solution)/shard_map/psum | solution.py:227
  8.5 10.9 %copy-start.18 = (s32[4,8,256]{2,1,0:T(8,128)S(1)}, s32[4,8,256]{2,1,0:T(8,128)}, u32[]{:S(2)}) copy-start(s32[4,8,256]{2,1,0:T(8,128)} %param.18) | copy-start | bytes 98308
  19.4 7.4 %copy-start.12 = (f32[4,8,256]{2,1,0:T(8,128)}, f32[4,8,256]{2,1,0:T(8,128)S(1)}, u32[]{:S(2)}) copy-start(f32[4,8,256]{2,1,0:T(8,128)S(1)} %multiply_convert_fusion.6) | copy-start | bytes 98308
  22.0 9.1 %copy-start.7 = (bf16[32,8,256]{2,1,0:T(8,128)(2,1)S(1)}, bf16[32,8,256]{2,1,0:T(8,128)(2,1)}, u32[]{:S(2)}) copy-start(bf16[32,8,256]{2,1,0:T(8,128)(2,1)} %param.12) | copy-start | bytes 393220
  27.7 7.3 %collective-permute-start = (f32[1,4,264]{2,1,0:T(4,128)S(1)}, f32[1,4,264]{2,1,0:T(4,128)S(1)}, u32[]{:S(2)}, u32[]{:S(2)}) collective-permute-start(f32[1,4,264]{2,1,0:T(4,128)S(1)} %get-tuple-element.260), channel_id=1, source_target_pairs={{0,16},{16,32},{32,48},{48,64},{64,80},{80,96},{96,112},{112,128},... | collective-permute-start | bytes 12680 | tf_op jit(solution)/shard_map/ppermute | solution.py:17
  30.3 4.7 collective-permute-start.1
  31.2 12.5 %copy-start.15 = (bf16[32,8,256]{2,1,0:T(8,128)(2,1)S(1)}, bf16[32,8,256]{2,1,0:T(8,128)(2,1)}, u32[]{:S(2)}) copy-start(bf16[32,8,256]{2,1,0:T(8,128)(2,1)} %param.13) | copy-start | bytes 393220
  31.2 14.6 %collective-permute-start.10 = (bf16[32,4,256]{2,1,0:T(4,128)(2,1)S(1)}, bf16[32,4,256]{2,1,0:T(4,128)(2,1)S(1)}, u32[]{:S(2)}, u32[]{:S(2)}) collective-permute-start(bf16[32,4,256]{2,1,0:T(4,128)(2,1)S(1)} %get-tuple-element.250), channel_id=1, source_target_pairs={{16,0},{32,16},{48,32},{64,48},{80,64},{96,80},{112,96},{128,112},... | collective-permute-start | bytes 196616 | tf_op jit(solution)/shard_map/ppermute | solution.py:20
  35.0 10.7 %collective-permute-start.9 = (bf16[32,4,256]{2,1,0:T(4,128)(2,1)S(1)}, bf16[32,4,256]{2,1,0:T(4,128)(2,1)S(1)}, u32[]{:S(2)}, u32[]{:S(2)}) collective-permute-start(bf16[32,4,256]{2,1,0:T(4,128)(2,1)S(1)} %get-tuple-element.249), channel_id=1, source_target_pairs={{0,16},{16,32},{32,48},{48,64},{64,80},{80,96},{96,112},{112,128},... | collective-permute-start | bytes 196616 | tf_op jit(solution)/shard_map/ppermute | solution.py:17
  35.1 8.3 %collective-permute-start.2 = (f32[1,24,4]{2,1,0:T(8,128)S(1)}, f32[1,24,4]{2,1,0:T(8,128)S(1)}, u32[]{:S(2)}, u32[]{:S(2)}) collective-permute-start(f32[1,24,4]{2,1,0:T(8,128)S(1)} %get-tuple-element.253), channel_id=1, source_target_pairs={{0,1},{1,2},{2,3},{3,4},{4,5},{5,6},{6,7},{7,8},{8,9},{9,10},{10,1... | collective-permute-start | bytes 1160 | tf_op jit(solution)/shard_map/ppermute | solution.py:17
  35.4 8.0 %collective-permute-start.3 = (f32[1,24,4]{2,1,0:T(8,128)S(1)}, f32[1,24,4]{2,1,0:T(8,128)S(1)}, u32[]{:S(2)}, u32[]{:S(2)}) collective-permute-start(f32[1,24,4]{2,1,0:T(8,128)S(1)} %get-tuple-element.254), channel_id=1, source_target_pairs={{1,0},{2,1},{3,2},{4,3},{5,4},{6,5},{7,6},{8,7},{9,8},{10,9},{11,1... | collective-permute-start | bytes 1160 | tf_op jit(solution)/shard_map/ppermute | solution.py:20
  43.6 0.6 copy-start.16
  44.3 7.3 %collective-permute-start.4 = (bf16[32,4,256]{2,1,0:T(4,128)(2,1)S(1)}, bf16[32,4,256]{2,1,0:T(4,128)(2,1)S(1)}, u32[]{:S(2)}, u32[]{:S(2)}) collective-permute-start(bf16[32,4,256]{2,1,0:T(4,128)(2,1)S(1)} %get-tuple-element.251), channel_id=1, source_target_pairs={{0,16},{16,32},{32,48},{48,64},{64,80},{80,96},{96,112},{112,128},... | collective-permute-start | bytes 196616 | tf_op jit(solution)/shard_map/ppermute | solution.py:17
  45.0 6.6 %collective-permute-start.5 = (bf16[32,4,256]{2,1,0:T(4,128)(2,1)S(1)}, bf16[32,4,256]{2,1,0:T(4,128)(2,1)S(1)}, u32[]{:S(2)}, u32[]{:S(2)}) collective-permute-start(bf16[32,4,256]{2,1,0:T(4,128)(2,1)S(1)} %get-tuple-element.252), channel_id=1, source_target_pairs={{16,0},{32,16},{48,32},{64,48},{80,64},{96,80},{112,96},{128,112},... | collective-permute-start | bytes 196616 | tf_op jit(solution)/shard_map/ppermute | solution.py:20
  46.0 24.8 %collective-permute-start.11 = (bf16[32,16,4]{2,1,0:T(8,128)(2,1)S(1)}, bf16[32,16,4]{2,1,0:T(8,128)(2,1)S(1)}, u32[]{:S(2)}, u32[]{:S(2)}) collective-permute-start(bf16[32,16,4]{2,1,0:T(8,128)(2,1)S(1)} %get-tuple-element.245), channel_id=1, source_target_pairs={{0,1},{1,2},{2,3},{3,4},{4,5},{5,6},{6,7},{7,8},{8,9},{9,10},{10,1... | collective-permute-start | bytes 12296 | tf_op jit(solution)/shard_map/ppermute | solution.py:17
  46.1 24.7 %collective-permute-start.12 = (bf16[32,16,4]{2,1,0:T(8,128)(2,1)S(1)}, bf16[32,16,4]{2,1,0:T(8,128)(2,1)S(1)}, u32[]{:S(2)}, u32[]{:S(2)}) collective-permute-start(bf16[32,16,4]{2,1,0:T(8,128)(2,1)S(1)} %get-tuple-element.246), channel_id=1, source_target_pairs={{1,0},{2,1},{3,2},{4,3},{5,4},{6,5},{7,6},{8,7},{9,8},{10,9},{11,1... | collective-permute-start | bytes 12296 | tf_op jit(solution)/shard_map/ppermute | solution.py:20
  51.9 18.9 %collective-permute-start.6 = (bf16[32,16,4]{2,1,0:T(8,128)(2,1)S(1)}, bf16[32,16,4]{2,1,0:T(8,128)(2,1)S(1)}, u32[]{:S(2)}, u32[]{:S(2)}) collective-permute-start(bf16[32,16,4]{2,1,0:T(8,128)(2,1)S(1)} %get-tuple-element.247), channel_id=1, source_target_pairs={{0,1},{1,2},{2,3},{3,4},{4,5},{5,6},{6,7},{7,8},{8,9},{9,10},{10,1... | collective-permute-start | bytes 12296 | tf_op jit(solution)/shard_map/ppermute | solution.py:17
  52.0 20.8 %collective-permute-start.7 = (bf16[32,16,4]{2,1,0:T(8,128)(2,1)S(1)}, bf16[32,16,4]{2,1,0:T(8,128)(2,1)S(1)}, u32[]{:S(2)}, u32[]{:S(2)}) collective-permute-start(bf16[32,16,4]{2,1,0:T(8,128)(2,1)S(1)} %get-tuple-element.248), channel_id=1, source_target_pairs={{1,0},{2,1},{3,2},{4,3},{5,4},{6,5},{7,6},{8,7},{9,8},{10,9},{11,1... | collective-permute-start | bytes 12296 | tf_op jit(solution)/shard_map/ppermute | solution.py:20
  74.5 5.3 %collective-permute-start.8 = (bf16[2,32,8,256]{3,2,1,0:T(8,128)(2,1)S(1)}, bf16[2,32,8,256]{3,2,1,0:T(8,128)(2,1)S(1)}, u32[]{:S(2)}, u32[]{:S(2)}) collective-permute-start(bf16[2,32,8,256]{3,2,1,0:T(8,128)(2,1)S(1)} %maximum_select_fusion.3), channel_id=1, source_target_pairs={{0,128},{16,144},{32,160},{48,176},{64,192},{80,208},{96,224},{112... | collective-permute-start | bytes 786440 | tf_op jit(solution)/shard_map/ppermute | solution.py:28
  75.8 6.8 %collective-permute-start.13 = (bf16[2,32,8,256]{3,2,1,0:T(8,128)(2,1)S(1)}, bf16[2,32,8,256]{3,2,1,0:T(8,128)(2,1)S(1)}, u32[]{:S(2)}, u32[]{:S(2)}) collective-permute-start(bf16[2,32,8,256]{3,2,1,0:T(8,128)(2,1)S(1)} %maximum_select_fusion.4), channel_id=1, source_target_pairs={{0,128},{16,144},{32,160},{48,176},{64,192},{80,208},{96,224},{112... | collective-permute-start | bytes 786440 | tf_op jit(solution)/shard_map/ppermute | solution.py:28
  83.2 1.0 copy-start
  83.2 1.0 copy-start.2
  83.2 1.0 copy-start.6
  84.2 1.0 copy-start.4
  99.7 1.0 copy-start.8
  100.9 4.2 copy-start.9
  115.4 1.2 copy-start.20
  119.5 1.0 copy-start.5
  120.4 1.0 copy-start.4
  135.9 1.0 copy-start.8
  137.1 4.2 copy-start.9
  151.7 1.2 copy-start.20
  155.8 1.0 copy-start.5
  156.7 9.6 %copy-start.1 = (f32[9,128,128]{2,1,0:T(8,128)}, f32[9,128,128]{2,1,0:T(8,128)S(1)}, u32[]{:S(2)}) copy-start(f32[9,128,128]{2,1,0:T(8,128)S(1)} %get-tuple-element.135) | copy-start | bytes 1769476
  156.7 9.6 %copy-start.3 = (f32[9,128,32]{1,2,0:T(8,128)}, f32[9,128,32]{1,2,0:T(8,128)S(1)}, u32[]{:S(2)}) copy-start(f32[9,128,32]{1,2,0:T(8,128)S(1)} %get-tuple-element.134) | copy-start | bytes 442372
  156.7 8.2 %collective-permute-start.14 = (f32[2,32,8,256]{3,2,1,0:T(8,128)}, f32[2,32,8,256]{3,2,1,0:T(8,128)S(1)}, u32[]{:S(2)}, u32[]{:S(2)}) collective-permute-start(f32[2,32,8,256]{3,2,1,0:T(8,128)} %get-tuple-element.133), channel_id=1, source_target_pairs={{0,128},{16,144},{32,160},{48,176},{64,192},{80,208},{96,224},{112... | collective-permute-start | bytes 1572872 | tf_op jit(solution)/shard_map/ppermute | solution.py:28
  166.3 0.8 copy-start.13
  199.6 11.8 %collective-permute-start.15 = (f32[32,4,264]{2,1,0:T(4,128)S(1)}, f32[32,4,264]{2,1,0:T(4,128)S(1)}, u32[]{:S(2)}, u32[]{:S(2)}) collective-permute-start(f32[32,4,264]{2,1,0:T(4,128)S(1)} %get-tuple-element.239), channel_id=1, source_target_pairs={{0,16},{16,32},{32,48},{48,64},{64,80},{80,96},{96,112},{112,128},... | collective-permute-start | bytes 405512 | tf_op jit(solution)/shard_map/ppermute | solution.py:17
  208.8 9.2 %collective-permute-start.16 = (f32[32,4,264]{2,1,0:T(4,128)S(1)}, f32[32,4,264]{2,1,0:T(4,128)S(1)}, u32[]{:S(2)}, u32[]{:S(2)}) collective-permute-start(f32[32,4,264]{2,1,0:T(4,128)S(1)} %get-tuple-element.240), channel_id=1, source_target_pairs={{16,0},{32,16},{48,32},{64,48},{80,64},{96,80},{112,96},{128,112},... | collective-permute-start | bytes 405512 | tf_op jit(solution)/shard_map/ppermute | solution.py:20
  218.3 16.7 %collective-permute-start.17 = (f32[32,24,4]{2,1,0:T(8,128)S(1)}, f32[32,24,4]{2,1,0:T(8,128)S(1)}, u32[]{:S(2)}, u32[]{:S(2)}) collective-permute-start(f32[32,24,4]{2,1,0:T(8,128)S(1)} %get-tuple-element.237), channel_id=1, source_target_pairs={{0,1},{1,2},{2,3},{3,4},{4,5},{5,6},{6,7},{7,8},{8,9},{9,10},{10,1... | collective-permute-start | bytes 36872 | tf_op jit(solution)/shard_map/ppermute | solution.py:17
  218.4 17.4 %collective-permute-start.18 = (f32[32,24,4]{2,1,0:T(8,128)S(1)}, f32[32,24,4]{2,1,0:T(8,128)S(1)}, u32[]{:S(2)}, u32[]{:S(2)}) collective-permute-start(f32[32,24,4]{2,1,0:T(8,128)S(1)} %get-tuple-element.238), channel_id=1, source_target_pairs={{1,0},{2,1},{3,2},{4,3},{5,4},{6,5},{7,6},{8,7},{9,8},{10,9},{11,1... | collective-permute-start | bytes 36872 | tf_op jit(solution)/shard_map/ppermute | solution.py:20
  235.0 0.8 copy-start.10
  235.7 0.7 copy-start.11
  236.7 0.9 slice-start
  236.7 1.0 slice-start.1
  236.7 1.0 copy-start.17
  488.3 2.0 copy-start.14
Sparse Core Ops, SparseCore 0:
  218.5 268.2 all-reduce.23
where the time goes:
time: 507 us; the launch traced here: 498 us
  waiting for transfers between devices  279 us (55%)
  starting transfers between devices  63.2 us (12%)
  matrix products  60.3 us (12%)
  local copies, waits for them, and re-layouts  53.6 us (11%)
  between operations  30.9 us (6%)
  other arithmetic  10.7 us (2%)
    psum x1, waiting for transfers between devices, shards(): summed_grads = lax.psum((totals[0], totals[1], totals[2]), ('lat', 'lon'))  248 us
    ppermute x8, starting transfers between devices, extended_2(): lax.ppermute(lax.slice_in_dim(block, 0, width, axis=dim), axis, backward)  47.8 us
    dynamic_update_slice x8, local copies, waits for them, and re-layouts, place_slots(): lax.dynamic_update_slice(canvas, current + per_slot[slot_index], corner)  34.6 us
    dot_general x54, matrix products, kernel_grad(): jnp.einsum('ohw,khw->ok', cotangent, padded[:, tap_row:tap_row + height,...  25.4 us
    dot_general x54, matrix products, forward_conv(): jnp.einsum('ok,khw->ohw', kernel[tap_index], padded[:, tap_row:tap_row +...  21.3 us
    dot_general x36, matrix products, backward_conv(): jnp.einsum('ok,ohw->khw', kernel[tap_index], padded[:, 2 - tap_row:2 - ta...  13.6 us
    ppermute x8, starting transfers between devices, extended_2(): lax.ppermute(lax.slice_in_dim(block, block.shape[dim] - width, None, axis...  13 us
    ppermute x3, waiting for transfers between devices, shifted(): return lax.ppermute(value, axis, pairs)  12.8 us
  transfers between devices with their start and end apart: 20, of which 9 were waited for; matrix products, arithmetic and copies ran while one was open for 1% of the time, Pallas kernels for 0%

commit v1 on v0

--- a/solution.py
+++ b/solution.py
@@ -224,7 +224,9 @@
     weighted = weights[:, None] * outputs
     numerator = fold_canvas(place_slots(weighted), keep_top, keep_bottom)
     blended = numerator / total_weight
-    summed_grads = lax.psum((totals[0], totals[1], totals[2]), ("lat", "lon"))
+    summed_grads = (totals[0], totals[1], totals[2])
+    for hop_no in ("lon", "lat"):
+        summed_grads = lax.psum(summed_grads, hop_no)
     return (blended, summed_grads[0], summed_grads[1], summed_grads[2])
 
 

time: 507 us -> 470 us (0.927)
  waiting for transfers between devices: 279 us -> 244 us
    psum x1 -> x2, waiting for transfers between devices: 248 us -> 212 us  [shards(): summed_grads = lax.psum(summed_grads, hop_no)]
  transfers between devices with their start and end apart: 20 -> 21, of which waited for: 9 -> 10; matrix products, arithmetic and copies ran while one was open for 1% -> 8% of each run, Pallas kernels for 0% -> 0%
where the time goes in v1:
time: 470 us; the launch traced here: 462 us
  waiting for transfers between devices  244 us (52%)
  starting transfers between devices  63.4 us (13%)
  matrix products  60.3 us (13%)
  local copies, waits for them, and re-layouts  52.9 us (11%)
  between operations  31 us (7%)
  other arithmetic  9.5 us (2%)
    psum x2, waiting for transfers between devices, shards(): summed_grads = lax.psum(summed_grads, hop_no)  212 us
    ppermute x8, starting transfers between devices, extended_2(): lax.ppermute(lax.slice_in_dim(block, 0, width, axis=dim), axis, backward)  47.8 us
    dynamic_update_slice x8, local copies, waits for them, and re-layouts, place_slots(): lax.dynamic_update_slice(canvas, current + per_slot[slot_index], corner)  34.6 us
    dot_general x54, matrix products, kernel_grad(): jnp.einsum('ohw,khw->ok', cotangent, padded[:, tap_row:tap_row + height,...  25.4 us
    dot_general x54, matrix products, forward_conv(): jnp.einsum('ok,khw->ohw', kernel[tap_index], padded[:, tap_row:tap_row +...  21.3 us
    dot_general x36, matrix products, backward_conv(): jnp.einsum('ok,ohw->khw', kernel[tap_index], padded[:, 2 - tap_row:2 - ta...  13.6 us
    ppermute x8, starting transfers between devices, extended_2(): lax.ppermute(lax.slice_in_dim(block, block.shape[dim] - width, None, axis...  13 us
    ppermute x3, waiting for transfers between devices, shifted(): return lax.ppermute(value, axis, pairs)  12.7 us
  transfers between devices with their start and end apart: 21, of which 10 were waited for; matrix products, arithmetic and copies ran while one was open for 8% of the time, Pallas kernels for 0%

profile of v1, /device:TPU:1, one launch (start us, length us, event | category | flops | bytes accessed | tf_op | source)
XLA Modules:
  0.0 461.6 jit_solution(6065262429663827356)
XLA Ops:
  27.9 2.6 collective-permute-start
  31.3 3.8 collective-permute-start.10
  35.5 7.0 %collective-permute-start.3 = (f32[1,24,4]{2,1,0:T(8,128)S(1)}, f32[1,24,4]{2,1,0:T(8,128)S(1)}, u32[]{:S(2)}, u32[]{:S(2)}) collective-permute-start(f32[1,24,4]{2,1,0:T(8,128)S(1)} %get-tuple-element.257), channel_id=1, source_target_pairs={{1,0},{2,1},{3,2},{4,3},{5,4},{6,5},{7,6},{8,7},{9,8},{10,9},{11,1... | collective-permute-start | bytes 1160 | tf_op jit(solution)/shard_map/ppermute | solution.py:20
  42.5 1.0 collective-permute-done.2
  46.3 5.5 %collective-permute-start.12 = (bf16[32,16,4]{2,1,0:T(8,128)(2,1)S(1)}, bf16[32,16,4]{2,1,0:T(8,128)(2,1)S(1)}, u32[]{:S(2)}, u32[]{:S(2)}) collective-permute-start(bf16[32,16,4]{2,1,0:T(8,128)(2,1)S(1)} %get-tuple-element.249), channel_id=1, source_target_pairs={{1,0},{2,1},{3,2},{4,3},{5,4},{6,5},{7,6},{8,7},{9,8},{10,9},{11,1... | collective-permute-start | bytes 12296 | tf_op jit(solution)/shard_map/ppermute | solution.py:20
  52.1 18.8 %collective-permute-start.7 = (bf16[32,16,4]{2,1,0:T(8,128)(2,1)S(1)}, bf16[32,16,4]{2,1,0:T(8,128)(2,1)S(1)}, u32[]{:S(2)}, u32[]{:S(2)}) collective-permute-start(bf16[32,16,4]{2,1,0:T(8,128)(2,1)S(1)} %get-tuple-element.251), channel_id=1, source_target_pairs={{1,0},{2,1},{3,2},{4,3},{5,4},{6,5},{7,6},{8,7},{9,8},{10,9},{11,1... | collective-permute-start | bytes 12296 | tf_op jit(solution)/shard_map/ppermute | solution.py:20
  71.0 1.9 collective-permute-done.7
  72.9 1.0 maximum_select_fusion.2
  76.9 3.1 collective-permute-done.8
  80.5 2.2 collective-permute-done.13
  84.4 72.5 %while.19 = (s32[]{:T(128)}, f32[9,128,32]{1,2,0:T(8,128)S(1)}, f32[9,128,128]{2,1,0:T(8,128)S(1)}, f32[9,32,128]{2,1,0:T(8,128)}, f32[2,32,8,256]{3,2,1,0:T(8,1...) while((s32[]{:T(128)}, f32[9,128,32]{1,2,0:T(8,128)S(1)}, ...), condition=%wide.region_1.3_spmd.clone, body=%wide.region_0.2_spmd.clone.sunk | while | flops 2583609344 | bytes 133587216 | solution.py:110
  84.4 1.0 constant_dynamic-slice_fusion.3
  88.8 1.5 multiply_convert_fusion.8
  101.1 0.8 fusion.448
  102.7 0.8 fusion.450
  103.6 0.9 fusion.451
  105.2 0.9 fusion.453
  106.1 0.8 fusion.454
  107.8 0.8 fusion.456
  108.6 1.6 select_add_fusion.8
  115.9 0.9 copy-done.21
  119.7 0.9 copy-done.5
  120.6 1.0 constant_dynamic-slice_fusion.3
  125.0 1.5 multiply_convert_fusion.8
  137.3 0.8 fusion.448
  138.9 0.8 fusion.450
  139.8 0.9 fusion.451
  141.5 0.9 fusion.453
  142.3 0.8 fusion.454
  144.0 0.8 fusion.456
  144.8 1.7 select_add_fusion.8
  152.2 0.9 copy-done.21
  156.0 0.9 copy-done.5
  157.9 7.4 %collective-permute-done.14 = f32[2,32,8,256]{3,2,1,0:T(8,128)S(1)} collective-permute-done((f32[2,32,8,256]{3,2,1,0:T(8,128)}, f32[2,32,8,256]{3,2,1,0:T(8,128)S(1)}, u32[]{:S(2)}, u32[]{:S(2)}) %collective-permute-start.14) | collective-permute-done | bytes 524320 | tf_op jit(solution)/shard_map/ppermute | solution.py:28
  166.3 10.2 %dynamic_update_slice.35 = f32[32,16,264]{2,1,0:T(8,128)S(1)} dynamic-update-slice(f32[32,16,264]{2,1,0:T(8,128)S(1)} %broadcast_in_dim.59, f32[32,8,256]{2,1,0:T(8,128)S(1)} %slice_bitcast_fusion.3, s32[]{:T(128)} %constant.84.clone.1, s32[]{:T(128)S(6)} %select_n.136, s32[]{:T(128)S(6)} %select_n.137) | dynamic-update-slice | bytes 524292 | tf_op jit(solution)/shard_map/dynamic_update_slice | solution.py:162
  176.6 10.2 %dynamic_update_slice.36 = f32[32,16,264]{2,1,0:T(8,128)S(1)} dynamic-update-slice(f32[32,16,264]{2,1,0:T(8,128)S(1)} %dynamic_update_slice.35, f32[32,8,256]{2,1,0:T(8,128)S(1)} %fusion.200, s32[]{:T(128)} %constant.84.clone.1, s32[]{:T(128)S(6)} %select_n.138, s32[]{:T(128)S(6)} %select_n.139) | dynamic-update-slice | bytes 524292 | tf_op jit(solution)/shard_map/dynamic_update_slice | solution.py:162
  187.0 1.3 dynamic_update_slice.37
  188.4 10.2 %dynamic_update_slice.38 = f32[32,16,264]{2,1,0:T(8,128)S(1)} dynamic-update-slice(f32[32,16,264]{2,1,0:T(8,128)S(1)} %dynamic_update_slice.37, f32[32,8,256]{2,1,0:T(8,128)S(1)} %fusion.198, s32[]{:T(128)} %constant.84.clone.1, s32[]{:T(128)S(6)} %select_n.142, s32[]{:T(128)S(6)} %select_n.143) | dynamic-update-slice | bytes 524292 | tf_op jit(solution)/shard_map/dynamic_update_slice | solution.py:162
  198.6 9.2 %collective-permute-start.15 = (f32[32,4,264]{2,1,0:T(4,128)S(1)}, f32[32,4,264]{2,1,0:T(4,128)S(1)}, u32[]{:S(2)}, u32[]{:S(2)}) collective-permute-start(f32[32,4,264]{2,1,0:T(4,128)S(1)} %get-tuple-element.242), channel_id=1, source_target_pairs={{0,16},{16,32},{32,48},{48,64},{64,80},{80,96},{96,112},{112,128},... | collective-permute-start | bytes 405512 | tf_op jit(solution)/shard_map/ppermute | solution.py:17
  207.8 2.6 collective-permute-done.15
  210.4 6.6 %collective-permute-done.16 = f32[32,4,264]{2,1,0:T(4,128)S(1)} collective-permute-done((f32[32,4,264]{2,1,0:T(4,128)S(1)}, f32[32,4,264]{2,1,0:T(4,128)S(1)}, u32[]{:S(2)}, u32[]{:S(2)}) %collective-permute-start.16) | collective-permute-done | bytes 135200 | tf_op jit(solution)/shard_map/ppermute | solution.py:20
  217.4 11.1 %collective-permute-start.18 = (f32[32,24,4]{2,1,0:T(8,128)S(1)}, f32[32,24,4]{2,1,0:T(8,128)S(1)}, u32[]{:S(2)}, u32[]{:S(2)}) collective-permute-start(f32[32,24,4]{2,1,0:T(8,128)S(1)} %get-tuple-element.241), channel_id=1, source_target_pairs={{1,0},{2,1},{3,2},{4,3},{5,4},{6,5},{7,6},{8,7},{9,8},{10,9},{11,1... | collective-permute-start | bytes 36872 | tf_op jit(solution)/shard_map/ppermute | solution.py:20
  228.5 7.0 %collective-permute-done.17 = f32[32,24,4]{2,1,0:T(8,128)S(1)} collective-permute-done((f32[32,24,4]{2,1,0:T(8,128)S(1)}, f32[32,24,4]{2,1,0:T(8,128)S(1)}, u32[]{:S(2)}, u32[]{:S(2)}) %collective-permute-start.17) | collective-permute-done | bytes 12320 | tf_op jit(solution)/shard_map/ppermute | solution.py:17
  236.4 77.1 %all-reduce.26.cloned.1.call-done = (f32[9,128,32]{1,2,0:T(8,128)}, f32[9,128,128]{2,1,0:T(8,128)}, f32[9,32,128]{2,1,0:T(8,128)}) async-done(((f32[9,128,32]{1,2,0:T(8,128)}, f32[9,128,128]{2,1,0:T(8,128)}, f32[9,32,128]{2,1,0:T(8,128)}), (f32[9,128,32]{1,2,0:T(8,128)}, f32[9,128,128]{2,1,0:T(8,128)}, f32[9,32,128]{2,1,0:T(8,128)})) %all-reduce.26.cloned.1.call-update) | async-done | bytes 884752 | tf_op jit(solution)/shard_map/psum | solution.py:229
  314.6 0.9 fusion.197
  315.5 134.6 %all-reduce.28.cloned.1.call-done = (f32[9,128,32]{1,2,0:T(8,128)}, f32[9,128,128]{2,1,0:T(8,128)}, f32[9,32,128]{2,1,0:T(8,128)}) async-done(((f32[9,128,32]{1,2,0:T(8,128)}, f32[9,128,128]{2,1,0:T(8,128)}, f32[9,32,128]{2,1,0:T(8,128)}), (f32[9,128,32]{1,2,0:T(8,128)}, f32[9,128,128]{2,1,0:T(8,128)}, f32[9,32,128]{2,1,0:T(8,128)})) %all-reduce.28.cloned.1.call-update) | async-done | bytes 884752 | tf_op jit(solution)/shard_map/psum | solution.py:229
  450.1 1.6 copy.286
  451.7 2.0 copy.287
  (288 shorter events, 68.8 us)
Async XLA Ops:
  7.2 306.2 %all-reduce.26.cloned.1.call-start = ((), (), s32[]{:S(2)}) async-start(), calls=%async_computation | async-start | bytes 1769472 | tf_op jit(solution)/shard_map/psum | solution.py:229
  8.5 10.9 %copy-start.19 = (s32[4,8,256]{2,1,0:T(8,128)S(1)}, s32[4,8,256]{2,1,0:T(8,128)}, u32[]{:S(2)}) copy-start(s32[4,8,256]{2,1,0:T(8,128)} %param.18) | copy-start | bytes 98308
  19.6 7.5 %copy-start.13 = (f32[4,8,256]{2,1,0:T(8,128)}, f32[4,8,256]{2,1,0:T(8,128)S(1)}, u32[]{:S(2)}) copy-start(f32[4,8,256]{2,1,0:T(8,128)S(1)} %multiply_convert_fusion.6) | copy-start | bytes 98308
  22.2 9.1 %copy-start.7 = (bf16[32,8,256]{2,1,0:T(8,128)(2,1)S(1)}, bf16[32,8,256]{2,1,0:T(8,128)(2,1)}, u32[]{:S(2)}) copy-start(bf16[32,8,256]{2,1,0:T(8,128)(2,1)} %param.12) | copy-start | bytes 393220
  27.9 7.3 %collective-permute-start = (f32[1,4,264]{2,1,0:T(4,128)S(1)}, f32[1,4,264]{2,1,0:T(4,128)S(1)}, u32[]{:S(2)}, u32[]{:S(2)}) collective-permute-start(f32[1,4,264]{2,1,0:T(4,128)S(1)} %get-tuple-element.263), channel_id=1, source_target_pairs={{0,16},{16,32},{32,48},{48,64},{64,80},{80,96},{96,112},{112,128},... | collective-permute-start | bytes 12680 | tf_op jit(solution)/shard_map/ppermute | solution.py:17
  30.5 4.7 %collective-permute-start.1 = (f32[1,4,264]{2,1,0:T(4,128)S(1)}, f32[1,4,264]{2,1,0:T(4,128)S(1)}, u32[]{:S(2)}, u32[]{:S(2)}) collective-permute-start(f32[1,4,264]{2,1,0:T(4,128)S(1)} %get-tuple-element.264), channel_id=1, source_target_pairs={{16,0},{32,16},{48,32},{64,48},{80,64},{96,80},{112,96},{128,112},... | collective-permute-start | bytes 12680 | tf_op jit(solution)/shard_map/ppermute | solution.py:20
  31.3 12.5 %copy-start.16 = (bf16[32,8,256]{2,1,0:T(8,128)(2,1)S(1)}, bf16[32,8,256]{2,1,0:T(8,128)(2,1)}, u32[]{:S(2)}) copy-start(bf16[32,8,256]{2,1,0:T(8,128)(2,1)} %param.13) | copy-start | bytes 393220
  31.3 14.6 %collective-permute-start.10 = (bf16[32,4,256]{2,1,0:T(4,128)(2,1)S(1)}, bf16[32,4,256]{2,1,0:T(4,128)(2,1)S(1)}, u32[]{:S(2)}, u32[]{:S(2)}) collective-permute-start(bf16[32,4,256]{2,1,0:T(4,128)(2,1)S(1)} %get-tuple-element.253), channel_id=1, source_target_pairs={{16,0},{32,16},{48,32},{64,48},{80,64},{96,80},{112,96},{128,112},... | collective-permute-start | bytes 196616 | tf_op jit(solution)/shard_map/ppermute | solution.py:20
  35.2 10.8 %collective-permute-start.9 = (bf16[32,4,256]{2,1,0:T(4,128)(2,1)S(1)}, bf16[32,4,256]{2,1,0:T(4,128)(2,1)S(1)}, u32[]{:S(2)}, u32[]{:S(2)}) collective-permute-start(bf16[32,4,256]{2,1,0:T(4,128)(2,1)S(1)} %get-tuple-element.252), channel_id=1, source_target_pairs={{0,16},{16,32},{32,48},{48,64},{64,80},{80,96},{96,112},{112,128},... | collective-permute-start | bytes 196616 | tf_op jit(solution)/shard_map/ppermute | solution.py:17
  35.2 8.3 %collective-permute-start.2 = (f32[1,24,4]{2,1,0:T(8,128)S(1)}, f32[1,24,4]{2,1,0:T(8,128)S(1)}, u32[]{:S(2)}, u32[]{:S(2)}) collective-permute-start(f32[1,24,4]{2,1,0:T(8,128)S(1)} %get-tuple-element.256), channel_id=1, source_target_pairs={{0,1},{1,2},{2,3},{3,4},{4,5},{5,6},{6,7},{7,8},{8,9},{9,10},{10,1... | collective-permute-start | bytes 1160 | tf_op jit(solution)/shard_map/ppermute | solution.py:17
  35.5 8.0 %collective-permute-start.3 = (f32[1,24,4]{2,1,0:T(8,128)S(1)}, f32[1,24,4]{2,1,0:T(8,128)S(1)}, u32[]{:S(2)}, u32[]{:S(2)}) collective-permute-start(f32[1,24,4]{2,1,0:T(8,128)S(1)} %get-tuple-element.257), channel_id=1, source_target_pairs={{1,0},{2,1},{3,2},{4,3},{5,4},{6,5},{7,6},{8,7},{9,8},{10,9},{11,1... | collective-permute-start | bytes 1160 | tf_op jit(solution)/shard_map/ppermute | solution.py:20
  44.4 7.3 %collective-permute-start.4 = (bf16[32,4,256]{2,1,0:T(4,128)(2,1)S(1)}, bf16[32,4,256]{2,1,0:T(4,128)(2,1)S(1)}, u32[]{:S(2)}, u32[]{:S(2)}) collective-permute-start(bf16[32,4,256]{2,1,0:T(4,128)(2,1)S(1)} %get-tuple-element.254), channel_id=1, source_target_pairs={{0,16},{16,32},{32,48},{48,64},{64,80},{80,96},{96,112},{112,128},... | collective-permute-start | bytes 196616 | tf_op jit(solution)/shard_map/ppermute | solution.py:17
  45.2 6.6 %collective-permute-start.5 = (bf16[32,4,256]{2,1,0:T(4,128)(2,1)S(1)}, bf16[32,4,256]{2,1,0:T(4,128)(2,1)S(1)}, u32[]{:S(2)}, u32[]{:S(2)}) collective-permute-start(bf16[32,4,256]{2,1,0:T(4,128)(2,1)S(1)} %get-tuple-element.255), channel_id=1, source_target_pairs={{16,0},{32,16},{48,32},{64,48},{80,64},{96,80},{112,96},{128,112},... | collective-permute-start | bytes 196616 | tf_op jit(solution)/shard_map/ppermute | solution.py:20
  46.2 24.8 %collective-permute-start.11 = (bf16[32,16,4]{2,1,0:T(8,128)(2,1)S(1)}, bf16[32,16,4]{2,1,0:T(8,128)(2,1)S(1)}, u32[]{:S(2)}, u32[]{:S(2)}) collective-permute-start(bf16[32,16,4]{2,1,0:T(8,128)(2,1)S(1)} %get-tuple-element.248), channel_id=1, source_target_pairs={{0,1},{1,2},{2,3},{3,4},{4,5},{5,6},{6,7},{7,8},{8,9},{9,10},{10,1... | collective-permute-start | bytes 12296 | tf_op jit(solution)/shard_map/ppermute | solution.py:17
  46.3 24.7 %collective-permute-start.12 = (bf16[32,16,4]{2,1,0:T(8,128)(2,1)S(1)}, bf16[32,16,4]{2,1,0:T(8,128)(2,1)S(1)}, u32[]{:S(2)}, u32[]{:S(2)}) collective-permute-start(bf16[32,16,4]{2,1,0:T(8,128)(2,1)S(1)} %get-tuple-element.249), channel_id=1, source_target_pairs={{1,0},{2,1},{3,2},{4,3},{5,4},{6,5},{7,6},{8,7},{9,8},{10,9},{11,1... | collective-permute-start | bytes 12296 | tf_op jit(solution)/shard_map/ppermute | solution.py:20
  52.0 18.9 %collective-permute-start.6 = (bf16[32,16,4]{2,1,0:T(8,128)(2,1)S(1)}, bf16[32,16,4]{2,1,0:T(8,128)(2,1)S(1)}, u32[]{:S(2)}, u32[]{:S(2)}) collective-permute-start(bf16[32,16,4]{2,1,0:T(8,128)(2,1)S(1)} %get-tuple-element.250), channel_id=1, source_target_pairs={{0,1},{1,2},{2,3},{3,4},{4,5},{5,6},{6,7},{7,8},{8,9},{9,10},{10,1... | collective-permute-start | bytes 12296 | tf_op jit(solution)/shard_map/ppermute | solution.py:17
  52.1 20.8 %collective-permute-start.7 = (bf16[32,16,4]{2,1,0:T(8,128)(2,1)S(1)}, bf16[32,16,4]{2,1,0:T(8,128)(2,1)S(1)}, u32[]{:S(2)}, u32[]{:S(2)}) collective-permute-start(bf16[32,16,4]{2,1,0:T(8,128)(2,1)S(1)} %get-tuple-element.251), channel_id=1, source_target_pairs={{1,0},{2,1},{3,2},{4,3},{5,4},{6,5},{7,6},{8,7},{9,8},{10,9},{11,1... | collective-permute-start | bytes 12296 | tf_op jit(solution)/shard_map/ppermute | solution.py:20
  74.6 5.3 %collective-permute-start.8 = (bf16[2,32,8,256]{3,2,1,0:T(8,128)(2,1)S(1)}, bf16[2,32,8,256]{3,2,1,0:T(8,128)(2,1)S(1)}, u32[]{:S(2)}, u32[]{:S(2)}) collective-permute-start(bf16[2,32,8,256]{3,2,1,0:T(8,128)(2,1)S(1)} %maximum_select_fusion.3), channel_id=1, source_target_pairs={{0,128},{16,144},{32,160},{48,176},{64,192},{80,208},{96,224},{112... | collective-permute-start | bytes 786440 | tf_op jit(solution)/shard_map/ppermute | solution.py:28
  76.0 6.8 %collective-permute-start.13 = (bf16[2,32,8,256]{3,2,1,0:T(8,128)(2,1)S(1)}, bf16[2,32,8,256]{3,2,1,0:T(8,128)(2,1)S(1)}, u32[]{:S(2)}, u32[]{:S(2)}) collective-permute-start(bf16[2,32,8,256]{3,2,1,0:T(8,128)(2,1)S(1)} %maximum_select_fusion.4), channel_id=1, source_target_pairs={{0,128},{16,144},{32,160},{48,176},{64,192},{80,208},{96,224},{112... | collective-permute-start | bytes 786440 | tf_op jit(solution)/shard_map/ppermute | solution.py:28
  83.4 1.0 copy-start
  83.4 1.0 copy-start.2
  83.4 1.0 copy-start.6
  84.4 1.0 copy-start.4
  99.8 1.0 copy-start.8
  101.1 4.2 copy-start.9
  115.6 1.2 copy-start.21
  119.6 1.0 copy-start.5
  120.6 1.0 copy-start.4
  136.1 1.0 copy-start.8
  137.3 4.2 copy-start.9
  151.9 1.2 copy-start.21
  155.9 1.0 copy-start.5
  156.9 0.9 copy-start.1
  156.9 0.9 copy-start.3
  156.9 8.3 %copy-start.10 = (f32[2,32,8,256]{3,2,1,0:T(8,128)S(1)}, f32[2,32,8,256]{3,2,1,0:T(8,128)}, u32[]{:S(2)}) copy-start(f32[2,32,8,256]{3,2,1,0:T(8,128)} %get-tuple-element.133) | copy-start | bytes 1572868
  156.9 8.3 %collective-permute-start.14 = (f32[2,32,8,256]{3,2,1,0:T(8,128)}, f32[2,32,8,256]{3,2,1,0:T(8,128)S(1)}, u32[]{:S(2)}, u32[]{:S(2)}) collective-permute-start(f32[2,32,8,256]{3,2,1,0:T(8,128)} %get-tuple-element.133), channel_id=1, source_target_pairs={{0,128},{16,144},{32,160},{48,176},{64,192},{80,208},{96,224},{112... | collective-permute-start | bytes 1572872 | tf_op jit(solution)/shard_map/ppermute | solution.py:28
  157.8 292.3 %all-reduce.28.cloned.1.call-start = ((), (), s32[]{:S(2)}) async-start(), calls=%async_computation.1 | async-start | bytes 1769472 | tf_op jit(solution)/shard_map/psum | solution.py:229
  165.3 0.8 copy-start.14
  198.6 11.8 %collective-permute-start.15 = (f32[32,4,264]{2,1,0:T(4,128)S(1)}, f32[32,4,264]{2,1,0:T(4,128)S(1)}, u32[]{:S(2)}, u32[]{:S(2)}) collective-permute-start(f32[32,4,264]{2,1,0:T(4,128)S(1)} %get-tuple-element.242), channel_id=1, source_target_pairs={{0,16},{16,32},{32,48},{48,64},{64,80},{80,96},{96,112},{112,128},... | collective-permute-start | bytes 405512 | tf_op jit(solution)/shard_map/ppermute | solution.py:17
  207.8 9.3 %collective-permute-start.16 = (f32[32,4,264]{2,1,0:T(4,128)S(1)}, f32[32,4,264]{2,1,0:T(4,128)S(1)}, u32[]{:S(2)}, u32[]{:S(2)}) collective-permute-start(f32[32,4,264]{2,1,0:T(4,128)S(1)} %get-tuple-element.243), channel_id=1, source_target_pairs={{16,0},{32,16},{48,32},{64,48},{80,64},{96,80},{112,96},{128,112},... | collective-permute-start | bytes 405512 | tf_op jit(solution)/shard_map/ppermute | solution.py:20
  217.3 18.3 %collective-permute-start.17 = (f32[32,24,4]{2,1,0:T(8,128)S(1)}, f32[32,24,4]{2,1,0:T(8,128)S(1)}, u32[]{:S(2)}, u32[]{:S(2)}) collective-permute-start(f32[32,24,4]{2,1,0:T(8,128)S(1)} %get-tuple-element.240), channel_id=1, source_target_pairs={{0,1},{1,2},{2,3},{3,4},{4,5},{5,6},{6,7},{7,8},{8,9},{9,10},{10,1... | collective-permute-start | bytes 36872 | tf_op jit(solution)/shard_map/ppermute | solution.py:17
  217.4 18.2 %collective-permute-start.18 = (f32[32,24,4]{2,1,0:T(8,128)S(1)}, f32[32,24,4]{2,1,0:T(8,128)S(1)}, u32[]{:S(2)}, u32[]{:S(2)}) collective-permute-start(f32[32,24,4]{2,1,0:T(8,128)S(1)} %get-tuple-element.241), channel_id=1, source_target_pairs={{1,0},{2,1},{3,2},{4,3},{5,4},{6,5},{7,6},{8,7},{9,8},{10,9},{11,1... | collective-permute-start | bytes 36872 | tf_op jit(solution)/shard_map/ppermute | solution.py:20
  235.6 0.8 copy-start.11
  235.6 77.9 %copy-start.12 = (f32[32,24,4]{2,1,0:T(8,128)}, f32[32,24,4]{2,1,0:T(8,128)S(1)}, u32[]{:S(2)}) copy-start(f32[32,24,4]{2,1,0:T(8,128)S(1)} %collective-permute-done.18) | copy-start | bytes 36868
  313.7 0.9 slice-start
  313.7 1.0 slice-start.1
  313.7 1.0 copy-start.18
  451.7 2.0 copy-start.15
  (2 other events, 1.3 us)
Sparse Core Ops, SparseCore 0:
  157.9 155.4 all-reduce.25
  316.3 133.8 all-reduce.27
